TPU v7x, 32 devices: a whole 2x2x4 slice. The times are simulated.
32 devices in a mesh: group: 2 (over y), seq: 4 (over z), req: 2 (over x), sub: 2 (over core).
Axes of the slice: x: 2, y: 2, z: 4, core: 2. Of those that a mesh axis runs over, the one named last changes fastest.
Arguments:
- latent_codes: bfloat16 [2, 16, 2048, 512], P(None, ('group', 'req', 'sub'), 'seq'), parts along dimension 1, may hold values from -6 to 6
- latent_scales: bfloat16 [2, 16, 2048, 4], P(None, ('group', 'req', 'sub'), 'seq'), parts along dimension 1, may hold values from 0.34 to 3.5
- rope_keys: bfloat16 [2, 16, 2048, 64], P(None, ('group', 'req', 'sub'), 'seq'), parts along dimension 1, may hold values from -6 to 6
- lengths: int32 [16], P(('group', 'req', 'sub')), parts along dimension 0, may hold values from 256 to 2048, as said below
- query_latent: bfloat16 [2, 16, 4, 128, 512], P(None, ('group', 'req', 'sub'), None, 'seq'), parts along dimension 1, may hold values from -64 to 64
- query_rope: bfloat16 [2, 16, 4, 128, 64], P(None, ('group', 'req', 'sub'), None, 'seq'), parts along dimension 1, may hold values from -8 to 8
- new_latent: bfloat16 [2, 16, 4, 512], P(None, ('group', 'req', 'sub')), parts along dimension 1, may hold values from -9 to 9
- new_rope: bfloat16 [2, 16, 4, 64], P(None, ('group', 'req', 'sub')), parts along dimension 1, may hold values from -6 to 6
Outputs:
- attended: bfloat16 [2, 16, 4, 128, 512], P(None, ('group', 'req', 'sub'), None, 'seq'), parts along dimension 1
- cache_codes: bfloat16 [2, 16, 512, 4, 512], P(None, ('group', 'req', 'sub'), None, 'seq'), parts along dimension 1
- cache_scales: bfloat16 [2, 16, 512, 4, 4], P(None, ('group', 'req', 'sub'), None, 'seq'), parts along dimension 1
- cache_rope: bfloat16 [2, 16, 512, 4, 64], P(None, ('group', 'req', 'sub'), None, 'seq'), parts along dimension 1
There are 2 independent parts, one for each index of `group`. A program takes and returns all parts, laid end to end along the dimension named above; each array names one. Nothing has to cross between parts.
Inputs may be any that keep to these rules, and one draw needn't show every extreme that they name: `lengths`: one request is exactly 2048 long.
All inputs are finite; a program needn't handle non-finite values.
Results may differ from a plain program's by a relative error of at most 0.013.
Values may be sent and summed in bfloat16 or wider, within the bound.
A program may use at most 64 MiB of HBM per device.

v0:
```python
import jax
import jax.numpy as jnp
from jax import lax
from jax.sharding import PartitionSpec as P

softmax_gain = 192.0 ** (-0.5)
masked_score = -1e30


def dequantize(code_values, scale_values):
    blocks = scale_values.shape[-1]
    latent_width = code_values.shape[-1]
    shaped = code_values.astype(jnp.float32).reshape(
        code_values.shape[:-1] + (blocks, latent_width // blocks)
    )
    scaled = shaped * scale_values.astype(jnp.float32)[..., None]
    return scaled.reshape(code_values.shape).astype(jnp.bfloat16)


def shard_partial(
    lat_query, rope_query, key_rows, rope_rows, usable, new_keys, new_rope_rows, holds_new
):
    tokens_new, head_count, latent_width = lat_query.shape
    query_rows = lat_query.reshape(tokens_new * head_count, latent_width)
    query_pos = rope_query.reshape(tokens_new * head_count, rope_query.shape[-1])
    scores = jnp.dot(query_rows, key_rows.T, preferred_element_type=jnp.float32)
    scores = (
        scores + jnp.dot(query_pos, rope_rows.T, preferred_element_type=jnp.float32)
    ) * softmax_gain
    fresh_scores = jnp.dot(query_rows, new_keys.T, preferred_element_type=jnp.float32)
    fresh_scores = (
        fresh_scores + jnp.dot(query_pos, new_rope_rows.T, preferred_element_type=jnp.float32)
    ) * softmax_gain
    token_of_row = jnp.arange(tokens_new * head_count, dtype=jnp.int32) // head_count
    causal = (jnp.arange(tokens_new, dtype=jnp.int32)[None, :] <= token_of_row[:, None]) & holds_new
    scores = jnp.where(usable[None, :], scores, masked_score)
    fresh_scores = jnp.where(causal, fresh_scores, masked_score)
    group_peak = jnp.maximum(jnp.max(scores, 1), jnp.max(fresh_scores, 1)).astype(jnp.bfloat16)
    peak_float = group_peak.astype(jnp.float32)[:, None]
    weights = jnp.where(usable[None, :], jnp.exp(scores - peak_float), 0.0).astype(jnp.bfloat16)
    fresh_weights = jnp.where(causal, jnp.exp(fresh_scores - peak_float), 0.0).astype(jnp.bfloat16)
    group_total = jnp.sum(weights.astype(jnp.float32), 1) + jnp.sum(
        fresh_weights.astype(jnp.float32), 1
    )
    group_sum = jnp.dot(weights, key_rows, preferred_element_type=jnp.float32)
    group_sum = group_sum + jnp.dot(fresh_weights, new_keys, preferred_element_type=jnp.float32)
    return (
        group_sum.astype(jnp.bfloat16).reshape(tokens_new, head_count, latent_width),
        group_peak.reshape(tokens_new, head_count),
        group_total.astype(jnp.bfloat16).reshape(tokens_new, head_count),
    )


def merge_groups(pieces):
    group_sum, group_peak, group_total = pieces
    peak_float = group_peak.astype(jnp.float32)
    overall = jnp.max(peak_float, 0)
    factor = jnp.exp(peak_float - overall)
    numerator = jnp.sum(factor[..., None] * group_sum.astype(jnp.float32), 0)
    denominator = jnp.sum(factor * group_total.astype(jnp.float32), 0)
    return (numerator / denominator[..., None]).astype(jnp.bfloat16)


def per_device(
    latent_codes, latent_scales, rope_keys, lengths, query_latent, query_rope, new_latent, new_rope
):
    shard_count = lax.axis_size("seq")
    seq_index = lax.axis_index("seq")
    layer_count, request_count, span, latent_width = latent_codes.shape
    lat_query, rope_query = (
        lax.all_gather(query_latent, "seq", axis=3, tiled=True),
        lax.all_gather(query_rope, "seq", axis=3, tiled=True),
    )

    def regroup_rows(values):
        return values.reshape(
            values.shape[0], values.shape[1], span // shard_count, shard_count, values.shape[-1]
        )

    codes_moved, scales_moved, rope_moved = (
        lax.all_to_all(regroup_rows(latent_codes), "seq", split_axis=3, concat_axis=2, tiled=True),
        lax.all_to_all(regroup_rows(latent_scales), "seq", split_axis=3, concat_axis=2, tiled=True),
        lax.all_to_all(regroup_rows(rope_keys), "seq", split_axis=3, concat_axis=2, tiled=True),
    )
    offsets = jnp.arange(span, dtype=jnp.int32)
    key_rows = dequantize(latent_codes, latent_scales)
    positions = seq_index * span + offsets
    usable = positions[None, :] < lengths[:, None]
    holds_new = seq_index == 0
    per_request = jax.vmap(shard_partial, in_axes=(0, 0, 0, 0, 0, 0, 0, None))
    per_layer = jax.vmap(per_request, in_axes=(0, 0, 0, 0, None, 0, 0, None))
    group_sum, group_peak, group_total = per_layer(
        lat_query, rope_query, key_rows, rope_keys, usable, new_latent, new_rope, holds_new
    )
    attended = merge_groups(
        (
            lax.all_to_all(group_sum[None], "seq", split_axis=4, concat_axis=0, tiled=True),
            lax.all_to_all(group_peak[None], "seq", split_axis=4, concat_axis=0, tiled=True),
            lax.all_to_all(group_total[None], "seq", split_axis=4, concat_axis=0, tiled=True),
        )
    )
    return (attended, codes_moved, scales_moved, rope_moved)


def solution(mesh):
    placed = (
        P(None, ("group", "req", "sub"), "seq", None),
        P(None, ("group", "req", "sub"), "seq", None),
        P(None, ("group", "req", "sub"), "seq", None),
        P(("group", "req", "sub")),
        P(None, ("group", "req", "sub"), None, "seq", None),
        P(None, ("group", "req", "sub"), None, "seq", None),
        P(None, ("group", "req", "sub"), None, None),
        P(None, ("group", "req", "sub"), None, None),
    )
    return jax.shard_map(
        per_device,
        mesh=mesh,
        in_specs=placed,
        out_specs=(
            P(None, ("group", "req", "sub"), None, "seq", None),
            P(None, ("group", "req", "sub"), None, "seq", None),
            P(None, ("group", "req", "sub"), None, "seq", None),
            P(None, ("group", "req", "sub"), None, "seq", None),
        ),
        check_vma=False,
    )
```

profile of v0, /device:TPU:0, one launch (start us, length us, event | category | flops | bytes accessed | tf_op | source)
XLA Modules:
  0.0 215.6 jit_solution(11127280630018597931)
XLA Ops:
  7.2 0.0 copy-start
  7.2 0.0 all-gather.2.cloned.1.call-start
  7.2 0.7 all-gather.2.cloned.1.call-update
  7.9 1.8 reshape.126
  9.8 0.8 copy.66
  10.6 6.3 %all-to-all-start.4 = ((bf16[2,2,128,4,4]{2,4,1,0,3:T(4,128)(2,1)}), bf16[2,2,128,4,4]{2,4,1,0,3:T(4,128)(2,1)S(1)}, u32[]{:S(2)}, u32[]{:S(2)}) async-start(bf16[2,2,128,4,4]{2,4,1,0,3:T(4,128)(2,1)} %copy.66), calls=%async_computation.4 | async-start | bytes 32768 | tf_op jit(solution)/shard_map/all_to_all | solution.py:82
  16.9 1.2 copy.68
  18.1 1.0 copy.69
  19.2 3.4 %all-to-all-done.4 = bf16[2,2,128,4,4]{2,4,1,0,3:T(4,128)(2,1)S(1)} async-done(((bf16[2,2,128,4,4]{2,4,1,0,3:T(4,128)(2,1)}), bf16[2,2,128,4,4]{2,4,1,0,3:T(4,128)(2,1)S(1)}, u32[]{:S(2)}, u32[]{:S(2)}) %all-to-all-start.4) | async-done | bytes 16416 | tf_op jit(solution)/shard_map/all_to_all | solution.py:82
  22.5 3.4 %all-to-all-start.5 = ((bf16[2,2,128,4,64]{2,4,1,0,3:T(8,128)(2,1)}), bf16[2,2,128,4,64]{2,4,1,0,3:T(8,128)(2,1)S(1)}, u32[]{:S(2)}, u32[]{:S(2)}) async-start(bf16[2,2,128,4,64]{2,4,1,0,3:T(8,128)(2,1)} %copy.69), calls=%async_computation.5 | async-start | bytes 524288 | tf_op jit(solution)/shard_map/all_to_all | solution.py:83
  25.9 1.0 copy.57
  26.9 3.9 %mul.38 = f32[2,2,512,4,128]{4,3,2,1,0:T(4,128)} broadcast(f32[2,2,512,4]{3,2,1,0:T(8,128)S(1)} %copy.57), dimensions={0,1,2,3} | broadcast | bytes 4227072 | tf_op jit(solution)/shard_map/mul | solution.py:16
  30.8 0.0 copy-start.2
  30.8 5.6 %mul.39 = f32[2,2,512,512]{3,2,1,0:T(8,128)} reshape(f32[2,2,512,4,128]{4,3,2,1,0:T(4,128)} %mul.38) | data formatting | bytes 8388608 | tf_op jit(solution)/shard_map/mul | solution.py:16
  36.4 0.0 copy-done.2
  36.4 2.2 %copy.63 = bf16[2,2,512,512]{3,1,2,0:T(2,128)(2,1)S(1)} copy(bf16[2,2,512,512]{3,2,1,0:T(8,128)(2,1)S(1)} %copy-done.2) | data formatting | bytes 4194304 | tf_op args[0]
  38.6 0.0 copy-start.4
  38.6 0.0 copy-start.6
  38.6 0.0 copy-start.5
  38.6 0.0 copy-start.3
  38.6 2.0 copy.64
  40.6 1.7 all-to-all-done.5
  42.3 4.5 %all-to-all-start.3 = ((bf16[2,2,128,4,512]{4,2,1,0,3:T(8,128)(2,1)}), bf16[2,2,128,4,512]{4,2,1,0,3:T(8,128)(2,1)}, u32[]{:S(2)}, u32[]{:S(2)}) async-start(bf16[2,2,128,4,512]{4,2,1,0,3:T(8,128)(2,1)} %copy.64), calls=%async_computation.3 | async-start | bytes 4194304 | tf_op jit(solution)/shard_map/all_to_all | solution.py:81
  46.8 0.0 copy-done.4
  46.8 71.2 %all_gather.7 = bf16[2,2,4,128,64]{4,3,2,1,0:T(8,128)(2,1)S(1)} all-gather(bf16[2,2,4,32,64]{4,3,2,1,0:T(8,128)(2,1)S(1)} %copy-done.4), channel_id=1, replica_groups=mesh['group'=2,'seq'=4,'req'=2,'sub'=2] {'seq'}, dimensions={3}, use_global_device_ids=true | all-gather | bytes 327680 | tf_op jit(solution)/shard_map/all_gather | solution.py:72
  118.0 0.0 copy-done.6
  118.0 0.1 broadcast_compare_fusion
  118.1 0.0 copy-done.5
  118.1 0.2 fusion.17
  118.3 0.0 copy-done.3
  118.3 2.8 %fusion.16 = f32[2,2,512,512]{2,3,1,0:T(8,128)} fusion(bf16[2,2,512,64]{3,2,1,0:T(8,128)(2,1)S(1)} %bitcast.77, bf16[2,2,512,64]{2,3,1,0:T(8,128)(2,1)S(1)} %copy-done.3), kind=kOutput, calls=%fused_computation.39 | convolution fusion | flops 134217728 | bytes 4718592 | tf_op jit(solution)/shard_map/vmap(vmap())/dot_general | solution.py:28
  121.1 0.0 all-gather.2.cloned.1.call-done
  121.1 0.0 copy-done
  121.1 2.3 %fusion.15 = (bf16[2,2,512]{2,1,0:T(2,128)(2,1)S(1)}, f32[2,2,512,4]{2,3,1,0:T(4,128)S(1)}) fusion(f32[2,2,512,4]{2,3,1,0:T(4,128)S(1)} %fusion.17, bf16[2,2,512,512]{3,2,1,0:T(8,128)(2,1)} %bitcast.74, bf16[2,2,4,512]{3,2,1,0:T(4,128)(2,1)S(1)} %copy-done, pred[512,4]{0,1:T(4,128)(4,1)S(1)} %fusion.8), kind=kOutput, calls=%fused_computation.38 | convolution fusion | flops 8419328 | bytes 2185216 | tf_op jit(solution)/shard_map/vmap(vmap())/dot_general | solution.py:30
  123.4 5.6 %fusion.14 = (bf16[2,2,512]{2,1,0:T(2,128)(2,1)S(1)}, f32[2,2,512,512]{2,3,1,0:T(8,128)S(1)}) fusion(f32[2,2,512,512]{2,3,1,0:T(8,128)} %fusion.16, bf16[2,2,512,512]{3,2,1,0:T(8,128)(2,1)} %bitcast.75, f32[2,2,512,512]{3,2,1,0:T(8,128)} %mul.39, bf16[2,2,512,512]{3,2,1,0:T(8,128)(2,1)S(1)} %copy-done.2, pred[2,512]{1,0:T(4,128)(4,1)S(1)} %broadcast_compare_fusion), kind=kOutput, calls=%fused_computation.37 | convolution fusion | flops 1081079808 | bytes 16782336 | tf_op jit(solution)/shard_map/vmap(vmap())/dot_general | solution.py:26
  128.9 0.0 copy-start.1
  129.0 1.9 copy-done.1
  130.9 0.7 convert_reduce_fusion
  131.7 0.2 copy.62
  131.9 0.8 reshape.135
  132.7 0.0 all-to-all-done.3
  132.7 5.0 %all-to-all-start.2 = ((bf16[4,2,256]{2,1,0:T(2,128)(2,1)}), bf16[4,2,256]{2,1,0:T(2,128)(2,1)S(1)}, u32[]{:S(2)}, u32[]{:S(2)}) async-start(bf16[4,2,256]{2,1,0:T(2,128)(2,1)} %reshape.135), calls=%async_computation.2 | async-start | bytes 8192 | tf_op jit(solution)/shard_map/all_to_all | solution.py:99
  137.6 7.1 %fusion.5 = f32[2,2,512,512]{3,2,1,0:T(8,128)} fusion(f32[2,2,512,512]{2,3,1,0:T(8,128)} %copy-done.1, f32[2,2,512]{2,1,0:T(2,128)S(1)} %get-tuple-element.20, pred[2,512]{1,0:T(4,128)(4,1)S(1)} %broadcast_compare_fusion, f32[2,2,512,512]{3,2,1,0:T(8,128)} %mul.39, bf16[2,2,512,512]{3,2,1,0:T(8,128)(2,1)S(1)} %copy-done.2), kind=kOutput, calls=%fused_computation.13 | convolution fusion | flops 1080033280 | bytes 14689280 | tf_op jit(solution)/shard_map/vmap(vmap())/dot_general | solution.py:45
  144.8 0.2 copy.59
  145.0 0.8 reshape.133
  145.7 0.0 all-to-all-done.2
  145.7 5.1 %all-to-all-start = ((bf16[4,2,256]{2,1,0:T(2,128)(2,1)}), bf16[4,2,256]{2,1,0:T(2,128)(2,1)S(1)}, u32[]{:S(2)}, u32[]{:S(2)}) async-start(bf16[4,2,256]{2,1,0:T(2,128)(2,1)} %reshape.133), calls=%async_computation | async-start | bytes 8192 | tf_op jit(solution)/shard_map/all_to_all | solution.py:98
  150.8 3.0 %add_convert_fusion = bf16[2,2,512,512]{3,2,1,0:T(8,128)(2,1)S(1)} fusion(f32[2,2,512,512]{3,2,1,0:T(8,128)} %fusion.5, bf16[2,2,4,512]{3,2,1,0:T(4,128)(2,1)S(1)} %copy-done, f32[2,2,512,4]{2,3,1,0:T(4,128)S(1)} %get-tuple-element.27, f32[2,2,512]{2,1,0:T(2,128)S(1)} %get-tuple-element.20, pred[512,4]{0,1:T(4,128)(4,1)S(1)} %fusion.8), kind=kOutput, calls=%fused_computation.6 | convolution fusion | flops 10510336 | bytes 6350848 | tf_op jit(solution)/shard_map/vmap(vmap())/dot_general | solution.py:46
  153.8 3.0 %copy.61 = bf16[1,2,2,4,128,512]{5,3,2,1,0,4:T(4,128)(2,1)} copy(bf16[1,2,2,4,128,512]{5,4,3,2,1,0:T(8,128)(2,1)S(1)} %bitcast.72) | data formatting | bytes 4194304 | tf_op jit(solution)/shard_map/broadcast_in_dim;vmap(vmap())/reshape | solution.py:97
  156.8 0.0 all-to-all-done
  156.8 5.1 %all-to-all-start.1 = ((bf16[1,2,2,4,128,512]{5,3,2,1,0,4:T(4,128)(2,1)}), bf16[1,2,2,4,128,512]{5,3,2,1,0,4:T(4,128)(2,1)S(1)}, u32[]{:S(2)}, u32[]{:S(2)}) async-start(bf16[1,2,2,4,128,512]{5,3,2,1,0,4:T(4,128)(2,1)} %copy.61), calls=%async_computation.1 | async-start | bytes 4194304 | tf_op jit(solution)/shard_map/all_to_all | solution.py:97
  161.9 0.6 copy_bitcast_fusion
  162.5 0.7 bitcast_bitcast_fusion
  163.2 3.1 %copy.65 = bf16[2,2,128,4,512]{4,2,3,1,0:T(8,128)(2,1)} copy(bf16[2,2,128,4,512]{4,2,1,0,3:T(8,128)(2,1)} %all-to-all-done.3) | data formatting | bytes 4194304 | tf_op jit(solution)/shard_map/all_to_all | solution.py:81
  166.3 0.3 reshape.134
  166.6 0.2 reduce_max.34
  166.8 0.3 reshape.136
  167.1 0.3 fusion.6
  167.4 38.4 %all-to-all-done.1 = bf16[1,2,2,4,128,512]{5,3,2,1,0,4:T(4,128)(2,1)S(1)} async-done(((bf16[1,2,2,4,128,512]{5,3,2,1,0,4:T(4,128)(2,1)}), bf16[1,2,2,4,128,512]{5,3,2,1,0,4:T(4,128)(2,1)S(1)}, u32[]{:S(2)}, u32[]{:S(2)}) %all-to-all-start.1) | async-done | bytes 2097184 | tf_op jit(solution)/shard_map/all_to_all | solution.py:97
  205.9 1.5 fusion
  207.4 0.3 divide_convert_fusion
  207.7 1.1 copy.71
  (9 shorter events, 0.1 us)
Async XLA Ops:
  7.2 113.9 %copy-start = (bf16[2,2,4,512]{3,2,1,0:T(4,128)(2,1)S(1)}, bf16[2,2,4,512]{3,2,1,0:T(4,128)(2,1)}, u32[]{:S(2)}) copy-start(bf16[2,2,4,512]{3,2,1,0:T(4,128)(2,1)} %param.14) | copy-start | bytes 49156
  7.2 113.9 %all-gather.2.cloned.1.call-start = ((), (), s32[]{:S(2)}) async-start(), calls=%async_computation.6 | async-start | bytes 2621440 | tf_op jit(solution)/shard_map/all_gather | solution.py:71
  10.6 11.9 %all-to-all-start.4 = ((bf16[2,2,128,4,4]{2,4,1,0,3:T(4,128)(2,1)}), bf16[2,2,128,4,4]{2,4,1,0,3:T(4,128)(2,1)S(1)}, u32[]{:S(2)}, u32[]{:S(2)}) async-start(bf16[2,2,128,4,4]{2,4,1,0,3:T(4,128)(2,1)} %copy.66), calls=%async_computation.4 | async-start | bytes 32768 | tf_op jit(solution)/shard_map/all_to_all | solution.py:82
  22.5 19.8 %all-to-all-start.5 = ((bf16[2,2,128,4,64]{2,4,1,0,3:T(8,128)(2,1)}), bf16[2,2,128,4,64]{2,4,1,0,3:T(8,128)(2,1)S(1)}, u32[]{:S(2)}, u32[]{:S(2)}) async-start(bf16[2,2,128,4,64]{2,4,1,0,3:T(8,128)(2,1)} %copy.69), calls=%async_computation.5 | async-start | bytes 524288 | tf_op jit(solution)/shard_map/all_to_all | solution.py:83
  30.8 5.6 %copy-start.2 = (bf16[2,2,512,512]{3,2,1,0:T(8,128)(2,1)S(1)}, bf16[2,2,512,512]{3,2,1,0:T(8,128)(2,1)}, u32[]{:S(2)}) copy-start(bf16[2,2,512,512]{3,2,1,0:T(8,128)(2,1)} %param.8) | copy-start | bytes 6291460
  38.6 8.2 %copy-start.4 = (bf16[2,2,4,32,64]{4,3,2,1,0:T(8,128)(2,1)S(1)}, bf16[2,2,4,32,64]{4,3,2,1,0:T(8,128)(2,1)}, u32[]{:S(2)}) copy-start(bf16[2,2,4,32,64]{4,3,2,1,0:T(8,128)(2,1)} %param.13) | copy-start | bytes 196612
  38.6 79.4 %copy-start.6 = (s32[2]{0:T(128)S(1)}, s32[2]{0:T(128)}, u32[]{:S(2)}) copy-start(s32[2]{0:T(128)} %param.11) | copy-start | bytes 28
  38.6 79.5 %copy-start.5 = (bf16[2,2,4,64]{3,2,1,0:T(4,128)(2,1)S(1)}, bf16[2,2,4,64]{3,2,1,0:T(4,128)(2,1)}, u32[]{:S(2)}) copy-start(bf16[2,2,4,64]{3,2,1,0:T(4,128)(2,1)} %param.15) | copy-start | bytes 6148
  38.6 79.7 %copy-start.3 = (bf16[2,2,512,64]{2,3,1,0:T(8,128)(2,1)S(1)}, bf16[2,2,512,64]{2,3,1,0:T(8,128)(2,1)}, u32[]{:S(2)}) copy-start(bf16[2,2,512,64]{2,3,1,0:T(8,128)(2,1)} %param.10) | copy-start | bytes 786436
  42.3 90.3 %all-to-all-start.3 = ((bf16[2,2,128,4,512]{4,2,1,0,3:T(8,128)(2,1)}), bf16[2,2,128,4,512]{4,2,1,0,3:T(8,128)(2,1)}, u32[]{:S(2)}, u32[]{:S(2)}) async-start(bf16[2,2,128,4,512]{4,2,1,0,3:T(8,128)(2,1)} %copy.64), calls=%async_computation.3 | async-start | bytes 4194304 | tf_op jit(solution)/shard_map/all_to_all | solution.py:81
  128.9 2.0 copy-start.1
  132.7 13.1 %all-to-all-start.2 = ((bf16[4,2,256]{2,1,0:T(2,128)(2,1)}), bf16[4,2,256]{2,1,0:T(2,128)(2,1)S(1)}, u32[]{:S(2)}, u32[]{:S(2)}) async-start(bf16[4,2,256]{2,1,0:T(2,128)(2,1)} %reshape.135), calls=%async_computation.2 | async-start | bytes 8192 | tf_op jit(solution)/shard_map/all_to_all | solution.py:99
  145.7 11.0 %all-to-all-start = ((bf16[4,2,256]{2,1,0:T(2,128)(2,1)}), bf16[4,2,256]{2,1,0:T(2,128)(2,1)S(1)}, u32[]{:S(2)}, u32[]{:S(2)}) async-start(bf16[4,2,256]{2,1,0:T(2,128)(2,1)} %reshape.133), calls=%async_computation | async-start | bytes 8192 | tf_op jit(solution)/shard_map/all_to_all | solution.py:98
  156.8 49.1 %all-to-all-start.1 = ((bf16[1,2,2,4,128,512]{5,3,2,1,0,4:T(4,128)(2,1)}), bf16[1,2,2,4,128,512]{5,3,2,1,0,4:T(4,128)(2,1)S(1)}, u32[]{:S(2)}, u32[]{:S(2)}) async-start(bf16[1,2,2,4,128,512]{5,3,2,1,0,4:T(4,128)(2,1)} %copy.61), calls=%async_computation.1 | async-start | bytes 4194304 | tf_op jit(solution)/shard_map/all_to_all | solution.py:97
Sparse Core Ops, SparseCore 0:
  9.6 73.4 all-gather.1
where the time goes:
time: 216 us
  blocking collectives  71.2 us (33%)
  waiting for transfers between devices  44.2 us (20%)
  local copies, waits for them, and re-layouts  32.4 us (15%)
  starting transfers between devices  29.4 us (14%)
  matrix products  20.9 us (10%)
  between operations  14.3 us (7%)
  other arithmetic  3.24 us (2%)
    all_gather x1, blocking collectives, per_device(): lax.all_gather(query_rope, 'seq', axis=3, tiled=True)  71.2 us
    all_to_all x1, waiting for transfers between devices, per_device(): lax.all_to_all(group_sum[None], 'seq', split_axis=4, concat_axis=0, tiled...  38.4 us
    mul x2, local copies, waits for them, and re-layouts, dequantize(): scaled = shaped * scale_values.astype(jnp.float32)[..., None]  9.47 us
    unnamed x22, local copies, waits for them, and re-layouts  9.29 us
    dot_general x1, matrix products, shard_partial(): group_sum = jnp.dot(weights, key_rows, preferred_element_type=jnp.float32)  7.14 us
    all_to_all x1, starting transfers between devices, per_device(): lax.all_to_all(regroup_rows(latent_scales), 'seq', split_axis=3, concat_a...  6.32 us
    reshape x4, local copies, waits for them, and re-layouts, regroup_rows(): values.reshape(values.shape[0], values.shape[1], span // shard_count, sha...  5.68 us
    dot_general x1, matrix products, shard_partial(): scores = jnp.dot(query_rows, key_rows.T, preferred_element_type=jnp.float32)  5.57 us
  transfers between devices with their start and end apart: 7, of which 3 were waited for; matrix products, arithmetic and copies ran while one was open for 24% of the time, Pallas kernels for 0%

commit v1 on v0

--- a/solution.py
+++ b/solution.py
@@ -5,6 +5,22 @@
 
 softmax_gain = 192.0 ** (-0.5)
 masked_score = -1e30
+
+
+def pairwise_exchange(value, axis, split, join):
+    ways, here = (lax.axis_size(axis), lax.axis_index(axis))
+    width = value.shape[split] // ways
+    lengths = list(value.shape)
+    lengths[split] = width
+    height = lengths[join]
+    lengths[join] = height * ways
+    full = jnp.zeros(lengths, value.dtype)
+    for mask in range(ways):
+        part = lax.dynamic_slice_in_dim(value, (here ^ mask) * width, width, axis=split)
+        if mask:
+            part = lax.ppermute(part, axis, [(d, d ^ mask) for d in range(ways)])
+        full = lax.dynamic_update_slice_in_dim(full, part, (here ^ mask) * height, axis=join)
+    return full
 
 
 def dequantize(code_values, scale_values):
@@ -79,7 +95,7 @@
 
     codes_moved, scales_moved, rope_moved = (
         lax.all_to_all(regroup_rows(latent_codes), "seq", split_axis=3, concat_axis=2, tiled=True),
-        lax.all_to_all(regroup_rows(latent_scales), "seq", split_axis=3, concat_axis=2, tiled=True),
+        pairwise_exchange(regroup_rows(latent_scales), "seq", 3, 2),
         lax.all_to_all(regroup_rows(rope_keys), "seq", split_axis=3, concat_axis=2, tiled=True),
     )
     offsets = jnp.arange(span, dtype=jnp.int32)

time: 216 us -> 261 us (1.21)
  the two profiles are of different devices: /device:TPU:0 before, /device:TPU:8 now
where the time goes in v1:
time: 261 us; the launch traced here: 260 us
  waiting for transfers between devices  80.4 us (31%)
  blocking collectives  76.8 us (29%)
  local copies, waits for them, and re-layouts  35.1 us (13%)
  starting transfers between devices  29.4 us (11%)
  matrix products  20.9 us (8%)
  between operations  14.3 us (5%)
  other arithmetic  3.25 us (1%)
    ppermute x3, waiting for transfers between devices, pairwise_exchange(): part = lax.ppermute(part, axis, [(d, d ^ mask) for d in range(ways)])  79.7 us
    all_gather x1, blocking collectives, per_device(): lax.all_gather(query_rope, 'seq', axis=3, tiled=True)  76.8 us
    mul x2, local copies, waits for them, and re-layouts, dequantize(): scaled = shaped * scale_values.astype(jnp.float32)[..., None]  9.47 us
    unnamed x26, local copies, waits for them, and re-layouts  9.3 us
    dot_general x1, matrix products, shard_partial(): group_sum = jnp.dot(weights, key_rows, preferred_element_type=jnp.float32)  7.16 us
    dot_general x1, matrix products, shard_partial(): scores = jnp.dot(query_rows, key_rows.T, preferred_element_type=jnp.float32)  5.57 us
    all_to_all x1, starting transfers between devices, per_device(): lax.all_to_all(regroup_rows(rope_keys), 'seq', split_axis=3, concat_axis=...  5.32 us
    all_to_all x1, starting transfers between devices, per_device(): lax.all_to_all(group_total[None], 'seq', split_axis=4, concat_axis=0, til...  5.27 us
  transfers between devices with their start and end apart: 9, of which 3 were waited for; matrix products, arithmetic and copies ran while one was open for 21% of the time, Pallas kernels for 0%

profile of v1, /device:TPU:8, one launch (start us, length us, event | category | flops | bytes accessed | tf_op | source)
XLA Modules:
  0.0 260.3 jit_solution(12269398816381501280)
XLA Ops:
  7.2 0.0 copy-start
  7.2 0.0 all-gather.2.cloned.1.call-start
  7.2 0.7 all-gather.2.cloned.1.call-update
  7.9 1.2 copy.80
  9.1 1.0 copy.81
  10.2 5.3 %all-to-all-start.4 = ((bf16[2,2,128,4,64]{2,4,1,0,3:T(8,128)(2,1)}), bf16[2,2,128,4,64]{2,4,1,0,3:T(8,128)(2,1)S(1)}, u32[]{:S(2)}, u32[]{:S(2)}) async-start(bf16[2,2,128,4,64]{2,4,1,0,3:T(8,128)(2,1)} %copy.81), calls=%async_computation.4 | async-start | bytes 524288 | tf_op jit(solution)/shard_map/all_to_all | solution.py:99
  15.5 1.0 copy.67
  16.5 3.8 %mul.50 = f32[2,2,512,4,128]{4,3,2,1,0:T(4,128)} broadcast(f32[2,2,512,4]{3,2,1,0:T(8,128)S(1)} %copy.67), dimensions={0,1,2,3} | broadcast | bytes 4227072 | tf_op jit(solution)/shard_map/mul | solution.py:32
  20.3 5.6 %mul.51 = f32[2,2,512,512]{3,2,1,0:T(8,128)} reshape(f32[2,2,512,4,128]{4,3,2,1,0:T(4,128)} %mul.50) | data formatting | bytes 8388608 | tf_op jit(solution)/shard_map/mul | solution.py:32
  25.9 0.0 copy-done.2
  25.9 2.2 copy.73
  28.1 0.0 copy-start.4
  28.1 0.0 copy-start.8
  28.1 0.0 copy-start.7
  28.1 0.0 copy-start.3
  28.1 2.0 copy.74
  30.1 0.0 all-to-all-done.4
  30.1 5.1 %all-to-all-start.3 = ((bf16[2,2,128,4,512]{4,2,1,0,3:T(8,128)(2,1)}), bf16[2,2,128,4,512]{4,2,1,0,3:T(8,128)(2,1)}, u32[]{:S(2)}, u32[]{:S(2)}) async-start(bf16[2,2,128,4,512]{4,2,1,0,3:T(8,128)(2,1)} %copy.74), calls=%async_computation.3 | async-start | bytes 4194304 | tf_op jit(solution)/shard_map/all_to_all | solution.py:97
  35.2 76.8 %all_gather.7 = bf16[2,2,4,128,64]{4,3,2,1,0:T(8,128)(2,1)S(1)} all-gather(bf16[2,2,4,32,64]{4,3,2,1,0:T(8,128)(2,1)S(1)} %copy-done.4), channel_id=1, replica_groups=mesh['group'=2,'seq'=4,'req'=2,'sub'=2] {'seq'}, dimensions={3}, use_global_device_ids=true | all-gather | bytes 327680 | tf_op jit(solution)/shard_map/all_gather | solution.py:88
  112.1 0.0 copy-done.8
  112.1 0.1 broadcast_compare_fusion
  112.2 0.2 fusion.17
  112.4 2.8 %fusion.16 = f32[2,2,512,512]{2,3,1,0:T(8,128)} fusion(bf16[2,2,512,64]{3,2,1,0:T(8,128)(2,1)S(1)} %bitcast.70, bf16[2,2,512,64]{2,3,1,0:T(8,128)(2,1)S(1)} %copy-done.3), kind=kOutput, calls=%fused_computation.46 | convolution fusion | flops 134217728 | bytes 4718592 | tf_op jit(solution)/shard_map/vmap(vmap())/dot_general | solution.py:44
  115.2 2.3 fusion.15
  117.4 5.6 %fusion.14 = (bf16[2,2,512]{2,1,0:T(2,128)(2,1)S(1)}, f32[2,2,512,512]{2,3,1,0:T(8,128)S(1)}) fusion(f32[2,2,512,512]{2,3,1,0:T(8,128)} %fusion.16, bf16[2,2,512,512]{3,2,1,0:T(8,128)(2,1)} %bitcast.68, f32[2,2,512,512]{3,2,1,0:T(8,128)} %mul.51, bf16[2,2,512,512]{3,2,1,0:T(8,128)(2,1)S(1)} %copy-done.2, pred[2,512]{1,0:T(4,128)(4,1)S(1)} %broadcast_compare_fusion), kind=kOutput, calls=%fused_computation.44 | convolution fusion | flops 1081079808 | bytes 16782336 | tf_op jit(solution)/shard_map/vmap(vmap())/dot_general | solution.py:42
  123.1 1.9 copy-done.1
  125.0 0.7 convert_reduce_fusion
  125.8 0.2 copy.72
  125.9 0.8 reshape.135
  126.7 0.0 all-to-all-done.3
  126.7 5.3 %all-to-all-start.2 = ((bf16[4,2,256]{2,1,0:T(2,128)(2,1)}), bf16[4,2,256]{2,1,0:T(2,128)(2,1)S(1)}, u32[]{:S(2)}, u32[]{:S(2)}) async-start(bf16[4,2,256]{2,1,0:T(2,128)(2,1)} %reshape.135), calls=%async_computation.2 | async-start | bytes 8192 | tf_op jit(solution)/shard_map/all_to_all | solution.py:115
  132.0 7.2 %fusion.5 = f32[2,2,512,512]{3,2,1,0:T(8,128)} fusion(f32[2,2,512,512]{2,3,1,0:T(8,128)} %copy-done.1, f32[2,2,512]{2,1,0:T(2,128)S(1)} %get-tuple-element.20, pred[2,512]{1,0:T(4,128)(4,1)S(1)} %broadcast_compare_fusion, f32[2,2,512,512]{3,2,1,0:T(8,128)} %mul.51, bf16[2,2,512,512]{3,2,1,0:T(8,128)(2,1)S(1)} %copy-done.2), kind=kOutput, calls=%fused_computation.13 | convolution fusion | flops 1080033280 | bytes 14689280 | tf_op jit(solution)/shard_map/vmap(vmap())/dot_general | solution.py:61
  139.2 0.2 copy.69
  139.4 0.8 reshape.133
  140.1 0.0 all-to-all-done.2
  140.1 5.1 %all-to-all-start = ((bf16[4,2,256]{2,1,0:T(2,128)(2,1)}), bf16[4,2,256]{2,1,0:T(2,128)(2,1)S(1)}, u32[]{:S(2)}, u32[]{:S(2)}) async-start(bf16[4,2,256]{2,1,0:T(2,128)(2,1)} %reshape.133), calls=%async_computation | async-start | bytes 8192 | tf_op jit(solution)/shard_map/all_to_all | solution.py:114
  145.2 2.9 %add_convert_fusion = bf16[2,2,512,512]{3,2,1,0:T(8,128)(2,1)S(1)} fusion(f32[2,2,512,512]{3,2,1,0:T(8,128)} %fusion.5, bf16[2,2,4,512]{3,2,1,0:T(4,128)(2,1)S(1)} %copy-done, f32[2,2,512,4]{2,3,1,0:T(4,128)S(1)} %get-tuple-element.31, f32[2,2,512]{2,1,0:T(2,128)S(1)} %get-tuple-element.20, pred[512,4]{0,1:T(4,128)(4,1)S(1)} %fusion.8), kind=kOutput, calls=%fused_computation.6 | convolution fusion | flops 10510336 | bytes 6350848 | tf_op jit(solution)/shard_map/vmap(vmap())/dot_general | solution.py:62
  148.2 0.0 copy-start.5
  148.2 3.0 %copy.71 = bf16[1,2,2,4,128,512]{5,3,2,1,0,4:T(4,128)(2,1)} copy(bf16[1,2,2,4,128,512]{5,4,3,2,1,0:T(8,128)(2,1)S(1)} %bitcast.65) | data formatting | bytes 4194304 | tf_op jit(solution)/shard_map/broadcast_in_dim;vmap(vmap())/reshape | solution.py:113
  151.2 0.0 all-to-all-done
  151.2 5.1 %all-to-all-start.1 = ((bf16[1,2,2,4,128,512]{5,3,2,1,0,4:T(4,128)(2,1)}), bf16[1,2,2,4,128,512]{5,3,2,1,0,4:T(4,128)(2,1)S(1)}, u32[]{:S(2)}, u32[]{:S(2)}) async-start(bf16[1,2,2,4,128,512]{5,3,2,1,0,4:T(4,128)(2,1)} %copy.71), calls=%async_computation.1 | async-start | bytes 4194304 | tf_op jit(solution)/shard_map/all_to_all | solution.py:113
  156.3 1.1 reshape.126
  157.4 1.8 constant_dynamic-slice_fusion
  159.2 0.0 collective-permute-start
  159.2 2.9 %collective-permute-start.1 = (bf16[2,2,128,1,4]{3,2,4,1,0:T(8,128)(2,1)}, bf16[2,2,128,1,4]{3,2,4,1,0:T(8,128)(2,1)}, u32[]{:S(2)}, u32[]{:S(2)}) collective-permute-start(bf16[2,2,128,1,4]{3,2,4,1,0:T(8,128)(2,1)} %get-tuple-element.23), channel_id=1, source_target_pairs={{0,8},{4,12},{8,0},{12,4},{1,9},{5,13},{9,1},{13,5},{2,10},{6,14},... | collective-permute-start | bytes 12296 | tf_op jit(solution)/shard_map/ppermute | solution.py:21
  162.1 0.6 collective-permute-start.2
  162.7 0.2 copy.76
  163.0 40.2 %collective-permute-done = bf16[2,2,128,1,4]{3,2,4,1,0:T(8,128)(2,1)} collective-permute-done((bf16[2,2,128,1,4]{3,2,4,1,0:T(8,128)(2,1)}, bf16[2,2,128,1,4]{3,2,4,1,0:T(8,128)(2,1)}, u32[]{:S(2)}, u32[]{:S(2)}) %collective-permute-start) | collective-permute-done | bytes 4128 | tf_op jit(solution)/shard_map/ppermute | solution.py:21
  203.2 1.3 copy.77
  204.4 31.9 %collective-permute-done.1 = bf16[2,2,128,1,4]{3,2,4,1,0:T(8,128)(2,1)} collective-permute-done((bf16[2,2,128,1,4]{3,2,4,1,0:T(8,128)(2,1)}, bf16[2,2,128,1,4]{3,2,4,1,0:T(8,128)(2,1)}, u32[]{:S(2)}, u32[]{:S(2)}) %collective-permute-start.1) | collective-permute-done | bytes 4128 | tf_op jit(solution)/shard_map/ppermute | solution.py:21
  236.4 1.3 copy.78
  237.6 7.6 %collective-permute-done.2 = bf16[2,2,128,1,4]{3,2,4,1,0:T(8,128)(2,1)S(1)} collective-permute-done((bf16[2,2,128,1,4]{3,2,4,1,0:T(8,128)(2,1)}, bf16[2,2,128,1,4]{3,2,4,1,0:T(8,128)(2,1)S(1)}, u32[]{:S(2)}, u32[]{:S(2)}) %collective-permute-start.2) | collective-permute-done | bytes 4128 | tf_op jit(solution)/shard_map/ppermute | solution.py:21
  245.2 0.2 copy.79
  245.5 0.0 copy-start.6
  245.5 0.7 bitcast_bitcast_fusion
  246.2 3.1 %copy.75 = bf16[2,2,128,4,512]{4,2,3,1,0:T(8,128)(2,1)} copy(bf16[2,2,128,4,512]{4,2,1,0,3:T(8,128)(2,1)} %all-to-all-done.3) | data formatting | bytes 4194304 | tf_op jit(solution)/shard_map/all_to_all | solution.py:97
  249.3 0.3 reshape.134
  249.6 0.2 reduce_max.34
  249.9 0.3 reshape.136
  250.2 0.3 fusion.6
  250.5 0.0 all-to-all-done.1
  250.5 1.5 fusion
  252.1 0.3 divide_convert_fusion
  252.3 1.1 copy.83
  (23 shorter events, 0.2 us)
Async XLA Ops:
  7.2 108.0 %copy-start = (bf16[2,2,4,512]{3,2,1,0:T(4,128)(2,1)S(1)}, bf16[2,2,4,512]{3,2,1,0:T(4,128)(2,1)}, u32[]{:S(2)}) copy-start(bf16[2,2,4,512]{3,2,1,0:T(4,128)(2,1)} %param.14) | copy-start | bytes 49156
  7.2 108.0 %all-gather.2.cloned.1.call-start = ((), (), s32[]{:S(2)}) async-start(), calls=%async_computation.5 | async-start | bytes 2621440 | tf_op jit(solution)/shard_map/all_gather | solution.py:87
  10.2 20.0 %all-to-all-start.4 = ((bf16[2,2,128,4,64]{2,4,1,0,3:T(8,128)(2,1)}), bf16[2,2,128,4,64]{2,4,1,0,3:T(8,128)(2,1)S(1)}, u32[]{:S(2)}, u32[]{:S(2)}) async-start(bf16[2,2,128,4,64]{2,4,1,0,3:T(8,128)(2,1)} %copy.81), calls=%async_computation.4 | async-start | bytes 524288 | tf_op jit(solution)/shard_map/all_to_all | solution.py:99
  20.3 5.6 %copy-start.2 = (bf16[2,2,512,512]{3,2,1,0:T(8,128)(2,1)S(1)}, bf16[2,2,512,512]{3,2,1,0:T(8,128)(2,1)}, u32[]{:S(2)}) copy-start(bf16[2,2,512,512]{3,2,1,0:T(8,128)(2,1)} %param.8) | copy-start | bytes 6291460
  28.1 7.1 %copy-start.4 = (bf16[2,2,4,32,64]{4,3,2,1,0:T(8,128)(2,1)S(1)}, bf16[2,2,4,32,64]{4,3,2,1,0:T(8,128)(2,1)}, u32[]{:S(2)}) copy-start(bf16[2,2,4,32,64]{4,3,2,1,0:T(8,128)(2,1)} %param.13) | copy-start | bytes 196612
  28.1 84.0 %copy-start.8 = (s32[2]{0:T(128)S(1)}, s32[2]{0:T(128)}, u32[]{:S(2)}) copy-start(s32[2]{0:T(128)} %param.11) | copy-start | bytes 28
  28.1 84.1 %copy-start.7 = (bf16[2,2,4,64]{3,2,1,0:T(4,128)(2,1)S(1)}, bf16[2,2,4,64]{3,2,1,0:T(4,128)(2,1)}, u32[]{:S(2)}) copy-start(bf16[2,2,4,64]{3,2,1,0:T(4,128)(2,1)} %param.15) | copy-start | bytes 6148
  28.1 84.3 %copy-start.3 = (bf16[2,2,512,64]{2,3,1,0:T(8,128)(2,1)S(1)}, bf16[2,2,512,64]{2,3,1,0:T(8,128)(2,1)}, u32[]{:S(2)}) copy-start(bf16[2,2,512,64]{2,3,1,0:T(8,128)(2,1)} %param.10) | copy-start | bytes 786436
  30.1 96.6 %all-to-all-start.3 = ((bf16[2,2,128,4,512]{4,2,1,0,3:T(8,128)(2,1)}), bf16[2,2,128,4,512]{4,2,1,0,3:T(8,128)(2,1)}, u32[]{:S(2)}, u32[]{:S(2)}) async-start(bf16[2,2,128,4,512]{4,2,1,0,3:T(8,128)(2,1)} %copy.74), calls=%async_computation.3 | async-start | bytes 4194304 | tf_op jit(solution)/shard_map/all_to_all | solution.py:97
  123.0 2.0 copy-start.1
  126.7 13.4 %all-to-all-start.2 = ((bf16[4,2,256]{2,1,0:T(2,128)(2,1)}), bf16[4,2,256]{2,1,0:T(2,128)(2,1)S(1)}, u32[]{:S(2)}, u32[]{:S(2)}) async-start(bf16[4,2,256]{2,1,0:T(2,128)(2,1)} %reshape.135), calls=%async_computation.2 | async-start | bytes 8192 | tf_op jit(solution)/shard_map/all_to_all | solution.py:115
  140.1 11.0 %all-to-all-start = ((bf16[4,2,256]{2,1,0:T(2,128)(2,1)}), bf16[4,2,256]{2,1,0:T(2,128)(2,1)S(1)}, u32[]{:S(2)}, u32[]{:S(2)}) async-start(bf16[4,2,256]{2,1,0:T(2,128)(2,1)} %reshape.133), calls=%async_computation | async-start | bytes 8192 | tf_op jit(solution)/shard_map/all_to_all | solution.py:114
  148.2 8.1 %copy-start.5 = (bf16[2,2,512,4]{2,3,1,0:T(4,128)(2,1)S(1)}, bf16[2,2,512,4]{2,3,1,0:T(4,128)(2,1)}, u32[]{:S(2)}) copy-start(bf16[2,2,512,4]{2,3,1,0:T(4,128)(2,1)} %param.9) | copy-start | bytes 49156
  151.2 99.3 %all-to-all-start.1 = ((bf16[1,2,2,4,128,512]{5,3,2,1,0,4:T(4,128)(2,1)}), bf16[1,2,2,4,128,512]{5,3,2,1,0,4:T(4,128)(2,1)S(1)}, u32[]{:S(2)}, u32[]{:S(2)}) async-start(bf16[1,2,2,4,128,512]{5,3,2,1,0,4:T(4,128)(2,1)} %copy.71), calls=%async_computation.1 | async-start | bytes 4194304 | tf_op jit(solution)/shard_map/all_to_all | solution.py:113
  159.2 43.9 %collective-permute-start = (bf16[2,2,128,1,4]{3,2,4,1,0:T(8,128)(2,1)}, bf16[2,2,128,1,4]{3,2,4,1,0:T(8,128)(2,1)}, u32[]{:S(2)}, u32[]{:S(2)}) collective-permute-start(bf16[2,2,128,1,4]{3,2,4,1,0:T(8,128)(2,1)} %get-tuple-element.24), channel_id=1, source_target_pairs={{0,4},{4,0},{8,12},{12,8},{1,5},{5,1},{9,13},{13,9},{2,6},{6,2},{1... | collective-permute-start | bytes 12296 | tf_op jit(solution)/shard_map/ppermute | solution.py:21
  159.2 77.1 %collective-permute-start.1 = (bf16[2,2,128,1,4]{3,2,4,1,0:T(8,128)(2,1)}, bf16[2,2,128,1,4]{3,2,4,1,0:T(8,128)(2,1)}, u32[]{:S(2)}, u32[]{:S(2)}) collective-permute-start(bf16[2,2,128,1,4]{3,2,4,1,0:T(8,128)(2,1)} %get-tuple-element.23), channel_id=1, source_target_pairs={{0,8},{4,12},{8,0},{12,4},{1,9},{5,13},{9,1},{13,5},{2,10},{6,14},... | collective-permute-start | bytes 12296 | tf_op jit(solution)/shard_map/ppermute | solution.py:21
  162.1 83.1 %collective-permute-start.2 = (bf16[2,2,128,1,4]{3,2,4,1,0:T(8,128)(2,1)}, bf16[2,2,128,1,4]{3,2,4,1,0:T(8,128)(2,1)S(1)}, u32[]{:S(2)}, u32[]{:S(2)}) collective-permute-start(bf16[2,2,128,1,4]{3,2,4,1,0:T(8,128)(2,1)} %get-tuple-element.22), channel_id=1, source_target_pairs={{0,12},{4,8},{8,4},{12,0},{1,13},{5,9},{9,5},{13,1},{2,14},{6,10},... | collective-permute-start | bytes 12296 | tf_op jit(solution)/shard_map/ppermute | solution.py:21
  245.5 6.6 %copy-start.6 = (bf16[2,2,512,1,4]{2,4,3,1,0:T(4,128)(2,1)}, bf16[2,2,512,1,4]{2,4,3,1,0:T(4,128)(2,1)S(1)}, u32[]{:S(2)}) copy-start(bf16[2,2,512,1,4]{2,4,3,1,0:T(4,128)(2,1)S(1)} %constant_dynamic-update-slice_fusion) | copy-start | bytes 49156
Sparse Core Ops, SparseCore 0:
  9.6 79.3 all-gather.1
